TPU v7x, 256 devices: a whole 4x4x8 slice. The times are simulated.
256 devices in a mesh: seq: 32 (over y, z_lo, core), head: 8 (over x, z_hi).
Axes of the slice: x: 4, y: 4, z: 8 (z_hi: 2, z_lo: 4; z = z_hi * 4 + z_lo), core: 2. Of those that a mesh axis runs over, the one named last changes fastest.
Arguments:
- queries: bfloat16 [4096, 8192], P('seq', 'head'), may hold values from -48 to 48
- keyval: bfloat16 [4096, 2048], P('seq', 'head'), may hold values from -48 to 48
- grad_out: bfloat16 [4096, 8192], P('seq', 'head'), may hold values from -6 to 6
- doc_ids: int32 [4096], P('seq'), may hold values from 0 to 3, never falling along the last dimension, each value on 1 to 2048 neighbouring positions
- deltas: bfloat16 [8, 4096, 8192], P('head', 'seq'), may hold values from -6 to 6
- node_weights: bfloat16 [8192, 2048], P('head', 'seq'), may hold values from -0.0625 to 0.0625
- layer_slot: int32 [8], replicated, may hold values from 0 to 7, each once
Outputs:
- grad_query: bfloat16 [4096, 8192], P('seq', 'head')
- grad_keyval: bfloat16 [4096, 2048], P('seq', 'head')
- scores: float32 [8, 16], replicated
Inputs may be any that keep to these rules, and one draw needn't show every extreme that they name: `layer_slot`: each of the 8 layers stands in exactly one slot. `doc_ids`: never falling along the sequence.
All inputs are finite; a program needn't handle non-finite values.
Results may differ from a plain program's by a relative error of at most 0.013.
Values may be sent and summed in bfloat16 or wider, within the bound.
A program may use at most 64 MiB of HBM per device.

v0:
```python
import math
import jax
import jax.numpy as jnp
from jax import lax
from jax.sharding import PartitionSpec as P

H = 64
KVH = 8
HD = 128


def over_blocks(step, carry, pieces):
    total_rows = pieces[0].shape[0]
    block_rows = 512

    def one_turn(turn_index, running):
        offset = turn_index * block_rows
        blocks = tuple((lax.dynamic_slice_in_dim(piece, offset, block_rows, 0) for piece in pieces))
        return step(running, *blocks, offset)

    return lax.fori_loop(0, total_rows // block_rows, one_turn, carry)


def on_device(queries, keyval, grad_out, doc_ids, deltas, node_weights, layer_slot):
    tok_rows = queries.shape[0]
    kv_local = keyval.shape[1] // (2 * HD)
    group_size = H // KVH
    score_scale = 1.0 / math.sqrt(HD)
    seq_total = tok_rows * lax.axis_size("seq")
    query_grid = queries.reshape(tok_rows, kv_local, group_size, HD)
    out_grid = grad_out.reshape(tok_rows, kv_local, group_size, HD)
    row_positions = lax.axis_index("seq") * tok_rows + jnp.arange(tok_rows, dtype=jnp.int32)

    def block_logits(kv_rows, key_ids, key_start):
        width = kv_rows.shape[0]
        kv_grid = kv_rows.reshape(width, kv_local, 2, HD)
        logits = (
            jnp.einsum(
                "tgie,rge->gitr", query_grid, kv_grid[:, :, 0], preferred_element_type=jnp.float32
            )
            * score_scale
        )
        key_positions = key_start + jnp.arange(width, dtype=jnp.int32)
        allowed = (key_ids[None, :] == doc_ids[:, None]) & (
            key_positions[None, :] <= row_positions[:, None]
        )
        return (logits, allowed, kv_grid)

    def forward_step(carry, kv_rows, key_ids, key_start):
        run_max, run_sum, accum = carry
        logits, allowed, kv_grid = block_logits(kv_rows, key_ids, key_start)
        new_max = jnp.maximum(run_max, jnp.max(jnp.where(allowed, logits, -1e30), axis=3))
        weights = jnp.where(allowed, jnp.exp(logits - new_max[..., None]), 0.0)
        factor = jnp.exp(run_max - new_max)
        run_sum = run_sum * factor + jnp.sum(weights, axis=3)
        values = kv_grid[:, :, 1].astype(jnp.float32)
        accum = accum * factor[..., None] + jnp.einsum(
            "gitr,rge->gite", weights, values, precision=lax.Precision.HIGHEST
        )
        return (new_max, run_sum, accum)

    stat_shape = (kv_local, group_size, tok_rows)
    forward_init = (
        jnp.full(stat_shape, -1e30, jnp.float32),
        jnp.zeros(stat_shape, jnp.float32),
        jnp.zeros(stat_shape + (HD,), jnp.float32),
    )
    run_max, run_sum, accum = over_blocks(
        forward_step,
        forward_init,
        (
            lax.all_gather(keyval, "seq", axis=0, tiled=True),
            lax.all_gather(doc_ids, "seq", axis=0, tiled=True),
        ),
    )
    log_total = run_max + jnp.log(run_sum)
    attn_out = accum / run_sum[..., None]
    row_dot = jnp.einsum(
        "tgie,gite->git", out_grid.astype(jnp.float32), attn_out, precision=lax.Precision.HIGHEST
    )

    def backward_step(carry, kv_rows, key_ids, key_start):
        query_accum = carry[0]
        width = kv_rows.shape[0]
        logits, allowed, kv_grid = block_logits(kv_rows, key_ids, key_start)
        probs = jnp.where(allowed, jnp.exp(logits - log_total[..., None]), 0.0)
        grad_probs = jnp.einsum(
            "tgie,rge->gitr", out_grid, kv_grid[:, :, 1], preferred_element_type=jnp.float32
        )
        grad_logits = (probs * (grad_probs - row_dot[..., None])).astype(jnp.bfloat16)
        query_accum = (
            query_accum
            + jnp.einsum(
                "gitr,rge->gite", grad_logits, kv_grid[:, :, 0], preferred_element_type=jnp.float32
            )
            * score_scale
        )
        probs_low = probs.astype(jnp.bfloat16)
        grad_keys = (
            jnp.einsum(
                "gitr,tgie->rge", grad_logits, query_grid, preferred_element_type=jnp.float32
            )
            * score_scale
        )
        grad_values = jnp.einsum(
            "gitr,tgie->rge", probs_low, out_grid, preferred_element_type=jnp.float32
        )
        block_grad = jnp.stack((grad_keys, grad_values), axis=2).reshape(width, kv_local * 2 * HD)
        kv_buffer = lax.dynamic_update_slice(
            carry[1], block_grad, (key_start, jnp.zeros((), jnp.int32))
        )
        return (query_accum, kv_buffer)

    query_zero = jnp.zeros(stat_shape + (HD,), jnp.float32)
    backward_init = (query_zero, jnp.zeros((seq_total, kv_local * 2 * HD), jnp.float32))
    backward_out = over_blocks(
        backward_step,
        backward_init,
        (
            lax.all_gather(keyval, "seq", axis=0, tiled=True),
            lax.all_gather(doc_ids, "seq", axis=0, tiled=True),
        ),
    )
    query_accum = backward_out[0]
    grad_query = (
        jnp.transpose(query_accum, (2, 0, 1, 3))
        .reshape(tok_rows, kv_local * group_size * HD)
        .astype(jnp.bfloat16)
    )
    grad_keyval = lax.psum_scatter(
        backward_out[1].astype(jnp.bfloat16), "seq", scatter_dimension=0, tiled=True
    )
    width_deltas = lax.all_to_all(deltas, "head", split_axis=2, concat_axis=0, tiled=True)
    grad_rows = lax.all_gather(grad_keyval, "head", axis=1, tiled=True)
    layer_count = width_deltas.shape[0]
    node_count = grad_rows.shape[1] // HD
    projected = jnp.einsum(
        "ltd,dc->ltc",
        width_deltas,
        lax.all_gather(node_weights, "seq", axis=1, tiled=True),
        preferred_element_type=jnp.float32,
    )
    grad_cols = grad_rows.astype(jnp.float32)
    per_column = jnp.sum(projected * grad_cols[None], axis=1)
    partial_value = jnp.sum(per_column.reshape(layer_count, node_count, HD), axis=2)
    totals = lax.psum(partial_value / math.sqrt(seq_total), ("seq", "head"))
    placing = (layer_slot[:, None] == jnp.arange(layer_count, dtype=jnp.int32)[None, :]).astype(
        jnp.float32
    )
    scores = jnp.dot(placing.T, totals, precision=lax.Precision.HIGHEST)
    return (grad_query, grad_keyval, scores)


def solution(mesh):
    return jax.shard_map(
        on_device,
        mesh=mesh,
        in_specs=(
            P("seq", "head"),
            P("seq", "head"),
            P("seq", "head"),
            P("seq"),
            P("head", "seq", None),
            P("head", "seq"),
            P(),
        ),
        out_specs=(P("seq", "head"), P("seq", "head"), P()),
        check_vma=False,
    )
```

profile of v0, /device:TPU:1, one launch (start us, length us, event | category | flops | bytes accessed | tf_op | source)
XLA Modules:
  0.0 491.0 jit_solution(3479772316284741002)
XLA Ops:
  7.2 1.6 copy.67
  12.0 1.7 copy.96
  13.7 46.0 %all-gather = s32[32,1,128]{2,1,0:T(1,128)S(1)} all-gather(s32[1,1,128]{2,1,0:T(1,128)S(1)} %bitcast.262), channel_id=1, replica_groups=mesh['seq'=32,'head'=8] {'seq'}, dimensions={0}, use_global_device_ids=true | all-gather | bytes 16896 | tf_op jit(solution)/shard_map/all_gather | solution.py:121
  59.7 18.1 %all-gather.4.cloned.1.call-done = bf16[4096,256]{0,1:T(8,128)(2,1)} async-done(((bf16[128,256]{0,1:T(8,128)(2,1)}), bf16[4096,256]{0,1:T(8,128)(2,1)}) %all-gather.4.cloned.1.call-update) | async-done | bytes 2097168 | tf_op jit(solution)/shard_map/all_gather | solution.py:120
  77.8 55.1 %while.34 = (s32[]{:T(128)}, f32[1,8,128]{2,1,0:T(8,128)S(1)}, f32[1,8,128]{2,1,0:T(8,128)S(1)}, f32[1,8,128,128]{3,2,1,0:T(8,128)}, s32[4096]{0:T(1024)S(1)}, /...) while((s32[]{:T(128)}, f32[1,8,128]{2,1,0:T(8,128)S(1)}, ...), condition=%wide.region_3.4_spmd.clone, body=%wide.region_0.3_spmd.clone.sunk | while | flops 945363584 | bytes 8728263 | solution.py:21
  79.1 1.4 fusion.67
  80.6 2.8 fusion.70
  86.6 3.8 fusion.70
  92.1 1.4 fusion.67
  93.6 3.8 fusion.70
  100.6 3.8 fusion.70
  107.6 3.8 fusion.70
  113.2 1.4 fusion.67
  114.6 3.8 fusion.70
  120.2 1.4 fusion.67
  121.7 3.8 fusion.70
  127.2 1.4 fusion.67
  128.7 3.8 fusion.70
  135.6 1.6 broadcast_in_dim.87.clone
  137.2 39.6 %while.35 = (s32[]{:T(128)}, f32[1,8,128,128]{3,2,1,0:T(8,128)S(1)}, bf16[4096,256]{1,0:T(8,128)(2,1)}, s32[4096]{0:T(1024)S(1)}, s32[128]{0:T(128)S(1)}, /*inde...) while((s32[]{:T(128)}, ...), condition=%wide.region_5.6_spmd.clone, body=%wide.region_4.5_spmd.clone.sunk | while | flops 675611264 | bytes 14438105 | solution.py:21
  178.3 6.9 %copy.73 = bf16[1,128,8192]{1,0,2:T(2,128)(2,1)} copy(bf16[1,128,8192]{2,1,0:T(8,128)(2,1)S(1)} %copy-done) | data formatting | bytes 4194304 | tf_op args[4]
  185.7 45.2 %reduce.8 = bf16[8192,128]{1,0:T(8,128)(2,1)S(1)} reduce(bf16[8192,1,128]{2,1,0:T(2,128)(2,1)} %bitcast.245, bf16[]{:T(256)} %broadcast.122), dimensions={1}, to_apply=%bitcast.163.reduce_sub_computation | reduce | bytes 4194306
  230.9 3.2 reshape.216
  234.1 54.8 %all_to_all.18 = bf16[8,2,65536]{2,1,0:T(2,128)(2,1)S(1)} all-to-all(bf16[8,2,65536]{2,1,0:T(2,128)(2,1)} %reshape.216), channel_id=1, replica_groups=mesh['seq'=32,'head'=8] {'head'}, dimensions={0} | all-to-all | bytes 4194304 | tf_op jit(solution)/shard_map/all_to_all | solution.py:133
  288.9 4.4 reshape.217
  293.3 2.5 copy.93
  295.8 2.6 copy.74
  299.4 31.5 %reduce-scatter.2.cloned.1.call-done = bf16[128,256]{1,0:T(8,128)(2,1)} async-done(((bf16[4096,256]{1,0:T(8,128)(2,1)}), bf16[128,256]{1,0:T(8,128)(2,1)}) %reduce-scatter.2.cloned.1.call-update) | async-done | bytes 65552 | tf_op jit(solution)/shard_map/reduce_scatter | solution.py:130
  330.9 42.4 %all_gather.17 = bf16[128,2048]{1,0:T(8,128)(2,1)S(1)} all-gather(bf16[128,256]{1,0:T(8,128)(2,1)} %reduce-scatter.2.cloned.1.call-done), channel_id=1, replica_groups=mesh['seq'=32,'head'=8] {'head'}, dimensions={1}, use_global_device_ids=true | all-gather | bytes 589824 | tf_op jit(solution)/shard_map/all_gather | solution.py:134
  374.4 26.8 %all-gather.6.cloned.1.call-done = bf16[1024,2048]{0,1:T(8,128)(2,1)} async-done(((bf16[1024,64]{0,1:T(8,128)(2,1)}), bf16[1024,2048]{0,1:T(8,128)(2,1)}) %all-gather.6.cloned.1.call-update) | async-done | bytes 4194320 | tf_op jit(solution)/shard_map/all_gather | solution.py:140
  401.1 7.2 %multiply_reduce_fusion = f32[8,2048]{1,0:T(8,128)S(1)} fusion(bf16[1024,2048]{0,1:T(8,128)(2,1)} %all-gather.6.cloned.1.call-done, f32[128,2048]{1,0:T(8,128)} %convert_element_type.38, bf16[1,128,8,1024]{3,1,2,0:T(8,128)(2,1)S(1)} %copy-done.1), kind=kOutput, calls=%fused_computation.60 | convolution fusion | flops 4299145216 | bytes 7405568 | tf_op jit(solution)/shard_map/ltd,dc->ltc/dot_general | solution.py:137
  408.4 75.2 %psum.7 = f32[8,16]{0,1:T(8,128)S(1)} all-reduce(f32[8,16]{0,1:T(8,128)S(1)} %broadcast_multiply_fusion), channel_id=1, replica_groups=mesh['seq'=32,'head'=8] {'seq','head'}, use_global_device_ids=true, to_apply=%region_9.10 | all-reduce | flops 128 | bytes 1024 | tf_op jit(solution)/shard_map/psum | solution.py:146
  (212 shorter events, 67.9 us)
Async XLA Ops:
  7.2 6.6 %copy-start.2 = (s32[128]{0:T(128)S(1)}, s32[128]{0:T(128)}, u32[]{:S(2)}) copy-start(s32[128]{0:T(128)} %param.14) | copy-start | bytes 1540
  7.2 70.7 %all-gather.4.cloned.1.call-start = ((), (), s32[]{:S(2)}) async-start(), calls=%async_computation.2 | async-start | bytes 2162688 | tf_op jit(solution)/shard_map/all_gather | solution.py:120
  8.8 322.0 %reduce-scatter.2.cloned.1.call-start = ((), (), s32[]{:S(2)}) async-start(), calls=%async_computation.3 | async-start | bytes 2162688 | tf_op jit(solution)/shard_map/reduce_scatter | solution.py:130
  176.8 1.6 copy-start
  176.8 224.4 %all-gather.6.cloned.1.call-start = ((), (), s32[]{:S(2)}) async-start(), calls=%async_computation.4 | async-start | bytes 4325376 | tf_op jit(solution)/shard_map/all_gather | solution.py:140
  298.4 102.7 %copy-start.1 = (bf16[1,128,8,1024]{3,1,2,0:T(8,128)(2,1)S(1)}, bf16[1,128,8,1024]{3,1,2,0:T(8,128)(2,1)}, u32[]{:S(2)}) copy-start(bf16[1,128,8,1024]{3,1,2,0:T(8,128)(2,1)} %copy.74) | copy-start | bytes 6291460
  374.4 109.2 %copy-start.3 = (s32[8]{0:T(128)S(1)}, s32[8]{0:T(128)}, u32[]{:S(2)}) copy-start(s32[8]{0:T(128)} %param.17) | copy-start | bytes 100
Sparse Core Ops, SparseCore 0:
  10.3 67.4 all-gather.3
  176.9 153.8 reduce-scatter.1
  332.7 68.3 all-gather.5
where the time goes:
time: 493 us; the launch traced here: 491 us
  blocking collectives  218 us (44%)
  waiting for transfers between devices  76.9 us (16%)
  matrix products  70.4 us (14%)
  other arithmetic  56.2 us (11%)
  local copies, waits for them, and re-layouts  53.6 us (11%)
  between operations  13.9 us (3%)
    psum x1, blocking collectives, on_device(): totals = lax.psum(partial_value / math.sqrt(seq_total), ('seq', 'head'))  75.2 us
    all_to_all x1, blocking collectives, on_device(): lax.all_to_all(deltas, 'head', split_axis=2, concat_axis=0, tiled=True)  54.8 us
    unnamed x6, other arithmetic  46.5 us
    all_gather x1, blocking collectives, on_device(): lax.all_gather(doc_ids, 'seq', axis=0, tiled=True)  46 us
    all_gather x1, blocking collectives, on_device(): grad_rows = lax.all_gather(grad_keyval, 'head', axis=1, tiled=True)  42.4 us
    reduce_scatter x1, waiting for transfers between devices, on_device(): lax.psum_scatter(backward_out[1].astype(jnp.bfloat16), 'seq', scatter_dim...  31.5 us
    dot_general x8, matrix products, forward_step(): jnp.einsum('gitr,rge->gite', weights, values, precision=lax.Precision.HIG...  29.4 us
    all_gather x1, waiting for transfers between devices, on_device(): lax.all_gather(node_weights, 'seq', axis=1, tiled=True)  26.8 us
  transfers between devices with their start and end apart: 3, of which 3 were waited for; matrix products, arithmetic and copies ran while one was open for 15% of the time, Pallas kernels for 0%

commit v1 on v0

--- a/solution.py
+++ b/solution.py
@@ -143,7 +143,8 @@
     grad_cols = grad_rows.astype(jnp.float32)
     per_column = jnp.sum(projected * grad_cols[None], axis=1)
     partial_value = jnp.sum(per_column.reshape(layer_count, node_count, HD), axis=2)
-    totals = lax.psum(partial_value / math.sqrt(seq_total), ("seq", "head"))
+    array_here = partial_value / math.sqrt(seq_total)
+    totals = lax.all_gather(array_here, ("seq", "head")).sum(axis=0)
     placing = (layer_slot[:, None] == jnp.arange(layer_count, dtype=jnp.int32)[None, :]).astype(
         jnp.float32
     )

time: 493 us -> 1090 us (2.21)
  blocking collectives: 218 us -> 814 us
    all_gather x0 -> x1, blocking collectives: none -> 671 us  [on_device(): totals = lax.all_gather(array_here, ('seq', 'head')).sum(axis=0)]
    psum x1 -> x0, blocking collectives: 75.2 us -> none  [on_device(): totals = lax.psum(partial_value / math.sqrt(seq_total), ('seq', 'head'))]
  transfers between devices with their start and end apart: 3 -> 3, of which waited for: 3 -> 3; matrix products, arithmetic and copies ran while one was open for 15% -> 7% of each run, Pallas kernels for 0% -> 0%
where the time goes in v1:
time: 1090 us
  blocking collectives  814 us (75%)
  waiting for transfers between devices  75.7 us (7%)
  matrix products  70.4 us (6%)
  other arithmetic  56.5 us (5%)
  local copies, waits for them, and re-layouts  53.7 us (5%)
  between operations  13.9 us (1%)
    all_gather x1, blocking collectives, on_device(): totals = lax.all_gather(array_here, ('seq', 'head')).sum(axis=0)  671 us
    all_to_all x1, blocking collectives, on_device(): lax.all_to_all(deltas, 'head', split_axis=2, concat_axis=0, tiled=True)  54.3 us
    unnamed x6, other arithmetic  46.5 us
    all_gather x1, blocking collectives, on_device(): lax.all_gather(doc_ids, 'seq', axis=0, tiled=True)  46 us
    all_gather x1, blocking collectives, on_device(): grad_rows = lax.all_gather(grad_keyval, 'head', axis=1, tiled=True)  42.8 us
    reduce_scatter x1, waiting for transfers between devices, on_device(): lax.psum_scatter(backward_out[1].astype(jnp.bfloat16), 'seq', scatter_dim...  33 us
    dot_general x8, matrix products, forward_step(): jnp.einsum('gitr,rge->gite', weights, values, precision=lax.Precision.HIG...  29.4 us
    unnamed x19, local copies, waits for them, and re-layouts  25.4 us
  transfers between devices with their start and end apart: 3, of which 3 were waited for; matrix products, arithmetic and copies ran while one was open for 7% of the time, Pallas kernels for 0%

profile of v1, /device:TPU:1, one launch (start us, length us, event | category | flops | bytes accessed | tf_op | source)
XLA Modules:
  0.0 1085.8 jit_solution(297777216696757390)
XLA Ops:
  7.2 1.6 copy.126
  12.0 1.7 copy.159
  13.7 46.0 %all-gather.1 = s32[32,1,128]{2,1,0:T(1,128)S(1)} all-gather(s32[1,1,128]{2,1,0:T(1,128)S(1)} %bitcast.264), channel_id=1, replica_groups=mesh['seq'=32,'head'=8] {'seq'}, dimensions={0}, use_global_device_ids=true | all-gather | bytes 16896 | tf_op jit(solution)/shard_map/all_gather | solution.py:121
  59.7 18.1 %all-gather.5.cloned.1.call-done = bf16[4096,256]{0,1:T(8,128)(2,1)} async-done(((bf16[128,256]{0,1:T(8,128)(2,1)}), bf16[4096,256]{0,1:T(8,128)(2,1)}) %all-gather.5.cloned.1.call-update) | async-done | bytes 2097168 | tf_op jit(solution)/shard_map/all_gather | solution.py:120
  77.8 55.1 %while.34 = (s32[]{:T(128)}, f32[1,8,128]{2,1,0:T(8,128)S(1)}, f32[1,8,128]{2,1,0:T(8,128)S(1)}, f32[1,8,128,128]{3,2,1,0:T(8,128)}, s32[4096]{0:T(1024)S(1)}, /...) while((s32[]{:T(128)}, f32[1,8,128]{2,1,0:T(8,128)S(1)}, ...), condition=%wide.region_3.4_spmd.clone, body=%wide.region_0.3_spmd.clone.sunk | while | flops 945363584 | bytes 8728263 | solution.py:21
  80.6 2.8 fusion.68
  85.1 1.4 fusion.65
  86.6 3.8 fusion.68
  93.6 3.8 fusion.68
  100.6 3.8 fusion.68
  106.2 1.4 fusion.65
  107.6 3.8 fusion.68
  113.2 1.4 fusion.65
  114.6 3.8 fusion.68
  120.2 1.4 fusion.65
  121.7 3.8 fusion.68
  127.2 1.4 fusion.65
  128.7 3.8 fusion.68
  135.6 1.6 broadcast_in_dim.87.clone
  137.2 39.6 %while.35 = (s32[]{:T(128)}, f32[1,8,128,128]{3,2,1,0:T(8,128)S(1)}, bf16[4096,256]{1,0:T(8,128)(2,1)}, s32[4096]{0:T(1024)S(1)}, s32[128]{0:T(128)S(1)}, /*inde...) while((s32[]{:T(128)}, ...), condition=%wide.region_5.6_spmd.clone, body=%wide.region_4.5_spmd.clone.sunk | while | flops 675611264 | bytes 14438105 | solution.py:21
  178.3 6.9 copy.132
  185.7 45.2 %reduce.8 = bf16[8192,128]{1,0:T(8,128)(2,1)S(1)} reduce(bf16[8192,1,128]{2,1,0:T(2,128)(2,1)} %bitcast.247, bf16[]{:T(256)} %broadcast.131), dimensions={1}, to_apply=%bitcast.165.reduce_sub_computation | reduce | bytes 4194306
  230.9 3.2 reshape.226
  234.1 54.3 %all_to_all.18 = bf16[8,2,65536]{2,1,0:T(2,128)(2,1)S(1)} all-to-all(bf16[8,2,65536]{2,1,0:T(2,128)(2,1)} %reshape.226), channel_id=1, replica_groups=mesh['seq'=32,'head'=8] {'head'}, dimensions={0} | all-to-all | bytes 4194304 | tf_op jit(solution)/shard_map/all_to_all | solution.py:133
  288.4 4.4 reshape.227
  292.8 2.5 copy.154
  295.3 2.6 copy.133
  298.9 33.0 %reduce-scatter.2.cloned.1.call-done = bf16[128,256]{1,0:T(8,128)(2,1)} async-done(((bf16[4096,256]{1,0:T(8,128)(2,1)}), bf16[128,256]{1,0:T(8,128)(2,1)}) %reduce-scatter.2.cloned.1.call-update) | async-done | bytes 65552 | tf_op jit(solution)/shard_map/reduce_scatter | solution.py:130
  331.9 42.8 %all_gather.21 = bf16[128,2048]{1,0:T(8,128)(2,1)S(1)} all-gather(bf16[128,256]{1,0:T(8,128)(2,1)} %reduce-scatter.2.cloned.1.call-done), channel_id=1, replica_groups=mesh['seq'=32,'head'=8] {'head'}, dimensions={1}, use_global_device_ids=true | all-gather | bytes 589824 | tf_op jit(solution)/shard_map/all_gather | solution.py:134
  375.9 24.0 %all-gather.7.cloned.1.call-done = bf16[1024,2048]{0,1:T(8,128)(2,1)} async-done(((bf16[1024,64]{0,1:T(8,128)(2,1)}), bf16[1024,2048]{0,1:T(8,128)(2,1)}) %all-gather.7.cloned.1.call-update) | async-done | bytes 4194320 | tf_op jit(solution)/shard_map/all_gather | solution.py:140
  399.8 7.2 multiply_reduce_fusion
  407.2 670.9 %all-gather = f32[2048,16]{1,0:T(8,128)S(1)} all-gather(f32[8,16]{1,0:T(8,128)S(1)} %broadcast_multiply_fusion), channel_id=2, replica_groups=mesh['seq'=32,'head'=8] {'seq','head'}, dimensions={0}, use_global_device_ids=true | all-gather | bytes 131584 | tf_op jit(solution)/shard_map/all_gather | solution.py:147
  (214 shorter events, 68.2 us)
Async XLA Ops:
  7.2 6.6 copy-start.2
  7.2 70.7 %all-gather.5.cloned.1.call-start = ((), (), s32[]{:S(2)}) async-start(), calls=%async_computation.2 | async-start | bytes 2162688 | tf_op jit(solution)/shard_map/all_gather | solution.py:120
  8.8 323.1 %reduce-scatter.2.cloned.1.call-start = ((), (), s32[]{:S(2)}) async-start(), calls=%async_computation.3 | async-start | bytes 2162688 | tf_op jit(solution)/shard_map/reduce_scatter | solution.py:130
  176.8 1.6 copy-start
  176.8 223.1 %all-gather.7.cloned.1.call-start = ((), (), s32[]{:S(2)}) async-start(), calls=%async_computation.4 | async-start | bytes 4325376 | tf_op jit(solution)/shard_map/all_gather | solution.py:140
  297.9 101.9 %copy-start.1 = (bf16[1,128,8,1024]{3,1,2,0:T(8,128)(2,1)S(1)}, bf16[1,128,8,1024]{3,1,2,0:T(8,128)(2,1)}, u32[]{:S(2)}) copy-start(bf16[1,128,8,1024]{3,1,2,0:T(8,128)(2,1)} %copy.133) | copy-start | bytes 6291460
  407.0 671.4 %copy-start.3 = (s32[8]{0:T(128)S(1)}, s32[8]{0:T(128)}, u32[]{:S(2)}) copy-start(s32[8]{0:T(128)} %param.17) | copy-start | bytes 100
Sparse Core Ops, SparseCore 0:
  10.3 67.4 all-gather.4
  176.9 154.9 reduce-scatter.1
  333.8 65.9 all-gather.6
